TPU v7x, 512 devices: a whole 4x4x16 slice. The times are simulated.
512 devices in a mesh: dp: 64 (over z_lo, x, core), expert: 8 (over z_hi, y).
Axes of the slice: x: 4, y: 4, z: 16 (z_hi: 2, z_lo: 8; z = z_hi * 8 + z_lo), core: 2. Of those that a mesh axis runs over, the one named last changes fastest.
Arguments:
- tokens: bfloat16 [768, 2048], P('dp', 'expert'), may hold values from -6 to 6
- cotangent: bfloat16 [768, 2048], P('dp', 'expert'), may hold values from -6 to 6
- route: int32 [768, 2], P('dp'), may hold values from 0 to 7, all different within a row; in each aligned block of 12 rows (0 to 11, 12 to 23, ...) at most 4 rows name the same one
- gates: float32 [768, 2], P('dp'), may hold values from 0.25 to 1
- w_gate: bfloat16 [8, 12288, 2048], P('expert', 'dp'), may hold values from -0.125 to 0.125
- w_up: bfloat16 [8, 12288, 2048], P('expert', 'dp'), may hold values from -0.125 to 0.125
- w_down: bfloat16 [8, 12288, 2048], P('expert', 'dp'), may hold values from -0.0546875 to 0.0546875
Outputs:
- mixed: bfloat16 [768, 2048], P('dp', 'expert')
- grad_tokens: bfloat16 [768, 2048], P('dp', 'expert')
- grad_gate: bfloat16 [8, 12288, 2048], P('expert', 'dp')
- grad_up: bfloat16 [8, 12288, 2048], P('expert', 'dp')
- grad_down: bfloat16 [8, 12288, 2048], P('expert', 'dp')
Inputs may be any that keep to these rules, and one draw needn't show every extreme that they name: `route`: the two experts of a token differ. Among the 12 tokens of one index of dp, at most 4 name the same expert, and in some such block one expert is named by exactly 4 tokens. Every expert is named by some token.
All inputs are finite; a program needn't handle non-finite values.
Results may differ from a plain program's by a relative error of at most 0.0065.
Values may be sent and summed in bfloat16 or wider, within the bound.
A program may use at most 64 MiB of HBM per device.

v0:
```python
import jax
import jax.numpy as jnp
from jax import lax
from jax.sharding import PartitionSpec as P


def contract_rows(left, right):
    return lax.dot_general(
        left, right, (((0,), (0,)), ((), ())), preferred_element_type=jnp.float32
    )


def contract_cols(left, right):
    return lax.dot_general(
        left, right, (((1,), (1,)), ((), ())), preferred_element_type=jnp.float32
    )


def apart_home(term_rows, capacity):
    summed = lax.psum_scatter(
        term_rows(jnp.int32(0), capacity * lax.axis_size("dp")),
        "dp",
        scatter_dimension=0,
        tiled=True,
    )
    return lax.all_to_all(
        summed.astype(jnp.bfloat16)[None], "expert", split_axis=2, concat_axis=0, tiled=True
    )


def per_device(tokens, cotangent, route, gates, w_gate, w_up, w_down):
    n_dp = lax.axis_size("dp")
    n_owner = lax.axis_size("expert")
    tok_rows = tokens.shape[0]
    feat_local = tokens.shape[1]
    full_width = feat_local * n_owner
    experts = w_gate.shape[0] * n_owner
    pairs = route.shape[1] * tok_rows
    capacity = min(tok_rows, max(2, 3 * tok_rows // experts))
    total_rows = n_dp * capacity
    assign = route.reshape(pairs)
    order = jnp.arange(pairs, dtype=jnp.int32)
    same = (assign[:, None] == assign[None, :]) & (order[None, :] < order[:, None])
    slot = jnp.sum(same.astype(jnp.int32), axis=1)
    expert_ids = jnp.arange(experts, dtype=jnp.int32)
    slot_ids = jnp.arange(capacity, dtype=jnp.int32)
    select = (
        (assign[None, None, :] == expert_ids[:, None, None])
        & (slot[None, None, :] == slot_ids[None, :, None])
    ).astype(jnp.bfloat16)
    gate_flat = gates.reshape(pairs)
    token_pairs = jnp.repeat(tokens, 2, axis=0)
    weighted = (gate_flat[:, None] * jnp.repeat(cotangent, 2, axis=0).astype(jnp.float32)).astype(
        jnp.bfloat16
    )
    send_tokens = jnp.einsum(
        "ecj,jd->ecd", select, token_pairs, preferred_element_type=jnp.float32
    ).astype(jnp.bfloat16)
    send_grads = jnp.einsum(
        "ecj,jd->ecd", select, weighted, preferred_element_type=jnp.float32
    ).astype(jnp.bfloat16)
    owned_tokens, owned_grads = (
        lax.all_to_all(send_tokens, "expert", split_axis=0, concat_axis=2, tiled=True),
        lax.all_to_all(send_grads, "expert", split_axis=0, concat_axis=2, tiled=True),
    )
    rows_tokens, rows_grads = (
        lax.all_gather(owned_tokens, "dp", axis=1, tiled=True),
        lax.all_gather(owned_grads, "dp", axis=1, tiled=True),
    )
    dys = rows_grads.reshape(total_rows, full_width)
    xs = rows_tokens.reshape(total_rows, full_width)
    w_g = w_gate[0]
    w_u = w_up[0]
    w_d = w_down[0]
    pre_gate = contract_cols(xs, w_g)
    pre_up = contract_cols(xs, w_u)
    sig = jax.nn.sigmoid(pre_gate)
    silu = pre_gate * sig
    hidden = (silu * pre_up).astype(jnp.bfloat16)

    def output_rows(start, count):
        return jnp.dot(hidden, w_d, preferred_element_type=jnp.float32)

    expert_home = apart_home(output_rows, capacity)
    grad_down = contract_rows(hidden, dys).astype(jnp.bfloat16)
    grad_hidden = contract_cols(dys, w_d)
    grad_pre_gate = (grad_hidden * pre_up * sig * (1.0 + pre_gate * (1.0 - sig))).astype(
        jnp.bfloat16
    )
    grad_pre_up = (grad_hidden * silu).astype(jnp.bfloat16)
    grad_gate = contract_rows(grad_pre_gate, xs).astype(jnp.bfloat16)
    grad_up = contract_rows(grad_pre_up, xs).astype(jnp.bfloat16)

    def input_rows(start, count):
        return jnp.dot(grad_pre_gate, w_g, preferred_element_type=jnp.float32) + jnp.dot(
            grad_pre_up, w_u, preferred_element_type=jnp.float32
        )

    grads_home = apart_home(input_rows, capacity)
    picked_out = jnp.einsum("ecj,ecd->jd", select, expert_home, preferred_element_type=jnp.float32)
    mixed = (
        (gate_flat[:, None] * picked_out)
        .reshape(tok_rows, 2, feat_local)
        .sum(axis=1)
        .astype(jnp.bfloat16)
    )
    picked_grad = jnp.einsum("ecj,ecd->jd", select, grads_home, preferred_element_type=jnp.float32)
    grad_tokens = picked_grad.reshape(tok_rows, 2, feat_local).sum(axis=1).astype(jnp.bfloat16)
    return (mixed, grad_tokens, grad_gate[None], grad_up[None], grad_down[None])


def solution(mesh):
    return jax.shard_map(
        per_device,
        mesh=mesh,
        in_specs=(
            P("dp", "expert"),
            P("dp", "expert"),
            P("dp", None),
            P("dp", None),
            P("expert", "dp", None),
            P("expert", "dp", None),
            P("expert", "dp", None),
        ),
        out_specs=(
            P("dp", "expert"),
            P("dp", "expert"),
            P("expert", "dp", None),
            P("expert", "dp", None),
            P("expert", "dp", None),
        ),
        check_vma=False,
    )
```

profile of v0, /device:TPU:8, one launch (start us, length us, event | category | flops | bytes accessed | tf_op | source)
XLA Modules:
  0.0 832.8 jit_solution(12606313329467337619)
XLA Ops:
  9.3 31.4 %all_to_all.72 = bf16[8,4,256]{2,1,0:T(4,128)(2,1)S(1)} all-to-all(bf16[8,4,256]{2,1,0:T(4,128)(2,1)S(1)} %copy.40), channel_id=1, replica_groups=mesh['dp'=64,'expert'=8] {'expert'}, dimensions={0} | all-to-all | bytes 32768 | tf_op jit(solution)/shard_map/all_to_all | solution.py:63
  43.2 17.3 %all_to_all.73 = bf16[8,4,256]{2,1,0:T(4,128)(2,1)S(1)} all-to-all(bf16[8,4,256]{2,1,0:T(4,128)(2,1)S(1)} %copy.45), channel_id=1, replica_groups=mesh['dp'=64,'expert'=8] {'expert'}, dimensions={0} | all-to-all | bytes 32768 | tf_op jit(solution)/shard_map/all_to_all | solution.py:64
  61.4 1.3 dynamic-slice
  64.0 91.5 %all-gather.3.cloned.1.call-done = bf16[1,256,2048]{2,0,1:T(2,128)(2,1)} async-done(((bf16[1,4,2048]{2,0,1:T(2,128)(2,1)}), bf16[1,256,2048]{2,0,1:T(2,128)(2,1)}) %all-gather.3.cloned.1.call-update) | async-done | bytes 1048592 | tf_op jit(solution)/shard_map/all_gather | solution.py:67
  155.5 2.2 copy.50
  157.7 1.2 fusion.10
  158.9 1.2 fusion.12
  160.0 114.6 %all-gather.5.cloned.1.call-done = bf16[1,256,2048]{2,0,1:T(2,128)(2,1)} async-done(((bf16[1,4,2048]{2,0,1:T(2,128)(2,1)}), bf16[1,256,2048]{2,0,1:T(2,128)(2,1)}) %all-gather.5.cloned.1.call-update) | async-done | bytes 1048592 | tf_op jit(solution)/shard_map/all_gather | solution.py:68
  274.6 2.5 multiply_convert_fusion
  277.2 1.3 fusion.1
  278.9 1.8 convolution_add_fusion
  280.7 1.8 fusion.15
  282.5 468.5 %all-reduce.4 = (bf16[256,2048]{1,0:T(8,128)(2,1)S(1)}, bf16[256,2048]{1,0:T(8,128)(2,1)}) all-reduce(f32[256,2048]{1,0:T(8,128)} %fusion.15, f32[256,2048]{1,0:T(8,128)} %convolution_add_fusion), channel_id=2, replica_groups=mesh['dp'=64,'expert'=8] {'dp'}, use_global_device_ids=true, to_apply=%region_1.0.clone | all-reduce | flops 1048576 | bytes 6291456
  753.1 11.5 %reduce = bf16[2048,4]{1,0:T(8,128)(2,1)S(1)} reduce(bf16[2048,1,4]{2,1,0:T(2,128)(2,1)S(1)} %bitcast.101, bf16[]{:T(256)} %broadcast.52), dimensions={1}, to_apply=%bitcast.86.reduce_sub_computation | reduce | bytes 32770
  764.7 1.4 reshape.103
  766.1 10.2 %all-to-all-start.1 = ((bf16[8,2,512]{2,1,0:T(2,128)(2,1)}), bf16[8,2,512]{2,1,0:T(2,128)(2,1)S(1)}, u32[]{:S(2)}, u32[]{:S(2)}) async-start(bf16[8,2,512]{2,1,0:T(2,128)(2,1)} %reshape.103), calls=%async_computation.1 | async-start | bytes 32768 | tf_op jit(solution)/shard_map/all_to_all | solution.py:26
  776.2 3.3 fusion.2
  779.6 1.3 fusion
  781.7 11.5 %reduce.1 = bf16[2048,4]{1,0:T(8,128)(2,1)S(1)} reduce(bf16[2048,1,4]{2,1,0:T(2,128)(2,1)S(1)} %bitcast.102, bf16[]{:T(256)} %broadcast.52), dimensions={1}, to_apply=%bitcast.88.reduce_sub_computation | reduce | bytes 32770
  793.2 1.4 reshape.105
  794.6 14.4 %all-to-all-start.3 = ((bf16[8,2,512]{2,1,0:T(2,128)(2,1)}), bf16[8,2,512]{2,1,0:T(2,128)(2,1)S(1)}, u32[]{:S(2)}, u32[]{:S(2)}) async-start(bf16[8,2,512]{2,1,0:T(2,128)(2,1)} %reshape.105), calls=%async_computation.3 | async-start | bytes 32768 | tf_op jit(solution)/shard_map/all_to_all | solution.py:26
  809.1 1.4 reshape.104
  811.3 11.3 %all-to-all-done.3 = bf16[8,2,512]{2,1,0:T(2,128)(2,1)S(1)} async-done(((bf16[8,2,512]{2,1,0:T(2,128)(2,1)}), bf16[8,2,512]{2,1,0:T(2,128)(2,1)S(1)}, u32[]{:S(2)}, u32[]{:S(2)}) %all-to-all-start.3) | async-done | bytes 16416 | tf_op jit(solution)/shard_map/all_to_all | solution.py:26
  822.5 1.4 reshape.106
  (45 shorter events, 12.4 us)
Async XLA Ops:
  7.2 267.5 %copy-start = (bf16[1,192,2048]{2,1,0:T(8,128)(2,1)S(1)}, bf16[1,192,2048]{2,1,0:T(8,128)(2,1)}, u32[]{:S(2)}) copy-start(bf16[1,192,2048]{2,1,0:T(8,128)(2,1)} %param.13) | copy-start | bytes 2359300
  7.2 150.5 %copy-start.1 = (bf16[1,192,2048]{2,1,0:T(8,128)(2,1)S(1)}, bf16[1,192,2048]{2,1,0:T(8,128)(2,1)}, u32[]{:S(2)}) copy-start(bf16[1,192,2048]{2,1,0:T(8,128)(2,1)} %param.12) | copy-start | bytes 2359300
  7.2 148.3 %all-gather.3.cloned.1.call-start = ((), (), s32[]{:S(2)}) async-start(), calls=%async_computation.4 | async-start | bytes 2129920 | tf_op jit(solution)/shard_map/all_gather | solution.py:67
  41.4 233.3 %all-gather.5.cloned.1.call-start = ((), (), s32[]{:S(2)}) async-start(), calls=%async_computation.5 | async-start | bytes 2129920 | tf_op jit(solution)/shard_map/all_gather | solution.py:68
  64.0 94.9 %copy-start.2 = (bf16[1,192,2048]{2,1,0:T(8,128)(2,1)S(1)}, bf16[1,192,2048]{2,1,0:T(8,128)(2,1)}, u32[]{:S(2)}) copy-start(bf16[1,192,2048]{2,1,0:T(8,128)(2,1)} %param.11) | copy-start | bytes 2359300
  277.2 3.5 copy-start.3
  766.1 28.6 %all-to-all-start.1 = ((bf16[8,2,512]{2,1,0:T(2,128)(2,1)}), bf16[8,2,512]{2,1,0:T(2,128)(2,1)S(1)}, u32[]{:S(2)}, u32[]{:S(2)}) async-start(bf16[8,2,512]{2,1,0:T(2,128)(2,1)} %reshape.103), calls=%async_computation.1 | async-start | bytes 32768 | tf_op jit(solution)/shard_map/all_to_all | solution.py:26
  794.6 27.9 %all-to-all-start.3 = ((bf16[8,2,512]{2,1,0:T(2,128)(2,1)}), bf16[8,2,512]{2,1,0:T(2,128)(2,1)S(1)}, u32[]{:S(2)}, u32[]{:S(2)}) async-start(bf16[8,2,512]{2,1,0:T(2,128)(2,1)} %reshape.105), calls=%async_computation.3 | async-start | bytes 32768 | tf_op jit(solution)/shard_map/all_to_all | solution.py:26
Sparse Core Ops, SparseCore 0:
  41.5 113.9 all-gather.2
  158.2 116.4 all-gather.4
where the time goes:
time: 833 us
  blocking collectives  517 us (62%)
  waiting for transfers between devices  217 us (26%)
  starting transfers between devices  24.7 us (3%)
  other arithmetic  24.6 us (3%)
  local copies, waits for them, and re-layouts  18.1 us (2%)
  matrix products  16 us (2%)
  between operations  14.8 us (2%)
    unnamed x1, blocking collectives  468 us
    all_gather x1, waiting for transfers between devices, per_device(): lax.all_gather(owned_grads, 'dp', axis=1, tiled=True)  115 us
    all_gather x1, waiting for transfers between devices, per_device(): lax.all_gather(owned_tokens, 'dp', axis=1, tiled=True)  91.5 us
    all_to_all x1, blocking collectives, per_device(): lax.all_to_all(send_tokens, 'expert', split_axis=0, concat_axis=2, tiled=...  31.4 us
    all_to_all x2, starting transfers between devices, apart_home(): lax.all_to_all(summed.astype(jnp.bfloat16)[None], 'expert', split_axis=2,...  24.6 us
    unnamed x2, other arithmetic  23.1 us
    all_to_all x1, blocking collectives, per_device(): lax.all_to_all(send_grads, 'expert', split_axis=0, concat_axis=2, tiled=T...  17.3 us
  transfers between devices with their start and end apart: 4, of which 3 were waited for; matrix products, arithmetic and copies ran while one was open for 4% of the time, Pallas kernels for 0%

commit v1 on v0

v1 whole, which is shorter than its diff:
```python
import functools

import jax
import jax.numpy as jnp
from jax import lax
from jax.experimental import pallas as pl
from jax.experimental.pallas import tpu as pltpu
from jax.sharding import PartitionSpec as P

MESH = pl.DeviceIdType.MESH
BF16 = jnp.bfloat16
F32 = jnp.float32
NX = 4
NC = 2
CAP = 4
ROWS = NX * CAP


def dot(left, right):
    return jnp.dot(left, right, preferred_element_type=F32)


def dot_cols(left, right):
    return lax.dot_general(left, right, (((1,), (1,)), ((), ())), preferred_element_type=F32)


def dot_rows(left, right):
    return lax.dot_general(left, right, (((0,), (0,)), ((), ())), preferred_element_type=F32)


def kernel(
    nz,
    ne,
    tok_ref,
    cot_ref,
    route_ref,
    gates_ref,
    wg_hbm,
    wu_hbm,
    wd_hbm,
    mixed_ref,
    gtok_ref,
    gg_hbm,
    gu_hbm,
    gd_hbm,
    snd,
    rcv,
    g,
    wg,
    wu,
    wd,
    acc,
    hid,
    part,
    sib,
    rel,
    full,
    zbuf,
    rz,
    snd2,
    rcv2,
    gg,
    gu,
    gd,
    w_sem,
    o_sem,
    send_sem,
    d_sem,
    z_sem,
    x_sem,
    c_sem,
    rs_sem,
    rz_sem,
    f_sem,
):
    p = lax.axis_index("dp")
    e = lax.axis_index("expert")
    zl = lax.div(p, NX * NC)
    x = lax.rem(lax.div(p, NC), NX)
    c = lax.rem(p, NC)
    right = lax.rem(x + 1, NX)
    left = lax.rem(x + 3, NX)
    opp = lax.rem(x + 2, NX)
    other = 1 - c
    e_half = lax.div(e, 2)
    e_par = lax.rem(e, 2)
    rows = nz * NC * ROWS
    feat = tok_ref.shape[1]
    chunk = 2 * feat
    toks = tok_ref.shape[0]

    def dp_of(z, xx, cc):
        return z * (NX * NC) + xx * NC + cc

    dev_right = (dp_of(zl, right, c), e)
    dev_left = (dp_of(zl, left, c), e)
    dev_sib = (dp_of(zl, x, other), e)
    sent = []

    def send(src, dst, rsem, device):
        copy = pltpu.make_async_remote_copy(
            src_ref=src,
            dst_ref=dst,
            send_sem=send_sem.at[len(sent)],
            recv_sem=rsem,
            device_id=device,
            device_id_type=MESH,
        )
        copy.start()
        sent.append(copy)

    def arrived(dst, rsem):
        pltpu.make_async_remote_copy(
            src_ref=dst,
            dst_ref=dst,
            send_sem=send_sem.at[0],
            recv_sem=rsem,
            device_id=dev_sib,
            device_id_type=MESH,
        ).wait_recv()

    barrier = pltpu.get_barrier_semaphore()

    def greet(dp, ex):
        pl.semaphore_signal(barrier, inc=1, device_id=(dp, ex), device_id_type=MESH)

    to_self = e_half == x
    for i in range(ne):

        @pl.when(jnp.logical_not(jnp.logical_and(to_self, e == i)))
        def _():
            greet(dp_of(zl, e_half, c), jnp.int32(i))

        xs_i, par_i = i // 2, i % 2

        @pl.when(jnp.logical_not(jnp.logical_and(x == xs_i, e == 2 * x + par_i)))
        def _():
            greet(dp_of(zl, jnp.int32(xs_i), c), 2 * x + par_i)

    for k in range(1, nz):
        greet(dp_of(lax.rem(zl + k, nz), x, c), e)
    greet(*dev_right)
    greet(*dev_left)
    greet(*dev_sib)

    loads = []
    for n, (hbm, vmem) in enumerate(((wg_hbm, wg), (wu_hbm, wu), (wd_hbm, wd))):
        for i in range(NX):
            copy = pltpu.make_async_copy(
                hbm.at[0, :, i * chunk : (i + 1) * chunk], vmem.at[i], w_sem.at[n * NX + i]
            )
            copy.start()
            loads.append(copy)

    lane = lax.broadcasted_iota(jnp.int32, (toks, ne * 2 * CAP), 1)
    lane_e = lane >> 3
    first = ((lane >> 2) & 1) == 0
    lane_c = (lane & 3).astype(F32)
    m0 = (route_ref[:, 0:1] == lane_e).astype(F32)
    m1 = (route_ref[:, 1:2] == lane_e).astype(F32)
    earlier = (
        lax.broadcasted_iota(jnp.int32, (toks, toks), 1)
        < lax.broadcasted_iota(jnp.int32, (toks, toks), 0)
    ).astype(F32)
    before = dot(earlier, m0 + m1)
    p0 = jnp.where(before == lane_c, m0, 0.0)
    p1 = jnp.where(before + m0 == lane_c, m1, 0.0)
    p0_out = jnp.where(first, p0, 0.0).astype(BF16)
    p1_out = jnp.where(first, p1, 0.0).astype(BF16)
    p0_grad = jnp.where(first, 0.0, p0).astype(BF16)
    p1_grad = jnp.where(first, 0.0, p1).astype(BF16)
    cot = cot_ref[...].astype(F32)
    weighted0 = (gates_ref[:, 0:1] * cot).astype(BF16)
    weighted1 = (gates_ref[:, 1:2] * cot).astype(BF16)
    placed = (
        dot_rows(p0_out + p1_out, tok_ref[...])
        + dot_rows(p0_grad, weighted0)
        + dot_rows(p1_grad, weighted1)
    )
    snd[...] = placed.reshape(ne, 2 * CAP, feat)

    pl.semaphore_wait(barrier, jnp.where(to_self, 2 * ne - 2, 2 * ne) + (nz - 1) + 3)

    def dispatch_copy(i):
        return pltpu.make_async_remote_copy(
            src_ref=snd.at[i],
            dst_ref=rcv.at[x * 2 + e_par],
            send_sem=d_sem.at[0, i],
            recv_sem=d_sem.at[1, x * 2 + e_par],
            device_id=(dp_of(zl, e_half, c), jnp.int32(i)),
            device_id_type=MESH,
        )

    for i in range(ne):
        mine = jnp.logical_and(to_self, e == i)

        @pl.when(mine)
        def _():
            rcv[x * 2 + e_par] = snd[i]

        @pl.when(jnp.logical_not(mine))
        def _():
            dispatch_copy(i).start()

    for i in range(ne):

        @pl.when(jnp.logical_not(jnp.logical_and(x == i // 2, e == 2 * x + i % 2)))
        def _():
            arrived(rcv.at[i], d_sem.at[1, i])

    sub = lax.broadcasted_iota(jnp.int32, (8, feat), 0) < CAP
    for par in range(2):
        t = [rcv[2 * i + par] for i in range(NX)]
        r = [pltpu.roll(v, CAP, 0) for v in t]
        cols = slice(par * feat, (par + 1) * feat)
        xs_rows = [jnp.where(sub, t[0], r[1]), jnp.where(sub, t[2], r[3])]
        dy_rows = [jnp.where(sub, r[0], t[1]), jnp.where(sub, r[2], t[3])]
        g[0, x, c, zl, :, cols] = jnp.concatenate(xs_rows, axis=0).astype(BF16)
        g[1, x, c, zl, :, cols] = jnp.concatenate(dy_rows, axis=0).astype(BF16)

    for k in range(1, nz):
        far = lax.rem(zl + k, nz)
        send(g.at[:, x, c, zl], g.at[:, x, c, zl], z_sem.at[zl], (dp_of(far, x, c), e))

    h = lax.div(zl, 2)
    pairs = [h, h + 1 - 2 * lax.rem(h, 2), lax.rem(h + 2, 4), 3 - h]

    def region(xi, cc, k):
        return g.at[:, xi, cc, pl.ds(2 * pairs[k], 2)]

    def half(a, xi, k):
        return g.at[a, xi, c, pl.ds(2 * pairs[k], 2)]

    def stage_a(k):
        if k == 0:
            z = zl + 1 - 2 * lax.rem(zl, 2)
            arrived(g.at[:, x, c, z], z_sem.at[z])
        else:
            for j in range(2):
                z = 2 * pairs[k] + j
                arrived(g.at[:, x, c, z], z_sem.at[z])
        send(region(x, c, k), region(x, c, k), x_sem.at[0, k], dev_right)
        send(region(x, c, k), region(x, c, k), x_sem.at[1, k], dev_left)
        send(region(x, c, k), region(x, c, k), c_sem.at[0, k], dev_sib)

    def stage_b(k):
        arrived(region(left, c, k), x_sem.at[0, k])
        send(half(0, left, k), half(0, left, k), x_sem.at[2, k], dev_right)
        send(region(left, c, k), region(left, c, k), c_sem.at[1, k], dev_sib)
        arrived(region(right, c, k), x_sem.at[1, k])
        send(half(1, right, k), half(1, right, k), x_sem.at[3, k], dev_left)
        send(region(right, c, k), region(right, c, k), c_sem.at[2, k], dev_sib)

    def stage_c(k):
        arrived(half(0, opp, k), x_sem.at[2, k])
        arrived(half(1, opp, k), x_sem.at[3, k])
        send(region(opp, c, k), region(opp, c, k), c_sem.at[3, k], dev_sib)

    for copy in loads:
        copy.wait()
    ng = nz // 2
    for k in range(ng + 2):
        if k < ng:
            stage_a(k)
        if 0 <= k - 1 < ng:
            stage_b(k - 1)
        if 0 <= k - 2 < ng:
            stage_c(k - 2)

    for n, xi in enumerate((x, left, right, opp)):
        for k in range(ng):
            arrived(region(xi, other, k), c_sem.at[n, k])
        xs = g[0, xi].reshape(rows, chunk)
        dys = g[1, xi].reshape(rows, chunk)
        terms = (dot_cols(xs, wg[xi]), dot_cols(xs, wu[xi]), dot_cols(dys, wd[xi]))
        for i in range(3):
            acc[i] = terms[i] if n == 0 else acc[i] + terms[i]

    pre_gate = acc[0]
    pre_up = acc[1]
    grad_hidden = acc[2]
    sig = jax.nn.sigmoid(pre_gate)
    silu = pre_gate * sig
    hid[0] = (silu * pre_up).astype(BF16)
    hid[1] = (grad_hidden * pre_up * sig * (1.0 + pre_gate * (1.0 - sig))).astype(BF16)
    hid[2] = (grad_hidden * silu).astype(BF16)

    for n, xi in enumerate((opp, right, left, x)):
        y0 = dot(hid[0], wd[xi])
        y1 = dot(hid[1], wg[xi]) + dot(hid[2], wu[xi])
        part[0, xi] = y0.astype(BF16).reshape(NC, nz, ROWS, chunk)
        part[1, xi] = y1.astype(BF16).reshape(NC, nz, ROWS, chunk)
        send(part.at[:, xi, other], sib.at[:, xi], rs_sem.at[n], dev_sib)

    def chip_sum(n, a, xi):
        return part[a, xi, c].astype(F32) + sib[a, xi].astype(F32)

    arrived(sib.at[:, opp], rs_sem.at[0])
    for a in range(2):
        part[a, opp, c] = chip_sum(0, a, opp).astype(BF16)
        send(part.at[a, opp, c], rel.at[a], rs_sem.at[4 + a], (dev_right, dev_left)[a])

    def weight_grad(n, left_rows, a, out, hbm):
        for i in range(NX):
            out[i] = dot_rows(left_rows, g[a, i].reshape(rows, chunk)).astype(BF16)
            copy = pltpu.make_async_copy(
                out.at[i], hbm.at[0, :, i * chunk : (i + 1) * chunk], o_sem.at[n * NX + i]
            )
            copy.start()
            loads.append(copy)

    del loads[:]
    weight_grad(0, hid[0], 1, gd, gd_hbm)

    for n, xi, device in ((0, right, dev_right), (1, left, dev_left)):
        arrived(sib.at[:, xi], rs_sem.at[1 + n])
        part[1 - n, xi, c] = chip_sum(1 + n, 1 - n, xi).astype(BF16)
        arrived(rel.at[n], rs_sem.at[4 + n])
        part[n, xi, c] = (chip_sum(1 + n, n, xi) + rel[n].astype(F32)).astype(BF16)
        send(part.at[:, xi, c], full.at[n], rs_sem.at[6 + n], device)

    weight_grad(1, hid[1], 0, gg, gg_hbm)
    weight_grad(2, hid[2], 0, gu, gu_hbm)

    arrived(sib.at[:, x], rs_sem.at[3])
    arrived(full.at[0], rs_sem.at[6])
    arrived(full.at[1], rs_sem.at[7])
    for a in range(2):
        total = chip_sum(3, a, x) + full[0, a].astype(F32) + full[1, a].astype(F32)
        zbuf[:, a] = total.astype(BF16)
    for k in range(1, nz):
        far = lax.rem(zl + k, nz)
        send(zbuf.at[far], rz.at[zl], rz_sem.at[zl], (dp_of(far, x, c), e))
    total = zbuf[zl].astype(F32)
    for k in range(1, nz):
        far = lax.rem(zl + k, nz)
        arrived(rz.at[far], rz_sem.at[far])
        total = total + rz[far].astype(F32)
    total = total.astype(BF16).astype(F32)

    for par in range(2):
        cols = slice(par * feat, (par + 1) * feat)
        for i in range(2):
            out_rows = total[0, 8 * i : 8 * i + 8, cols]
            grad_rows = total[1, 8 * i : 8 * i + 8, cols]
            snd2[4 * i + par] = jnp.where(sub, out_rows, pltpu.roll(grad_rows, CAP, 0))
            snd2[4 * i + 2 + par] = jnp.where(sub, pltpu.roll(out_rows, CAP, 0), grad_rows)

    def return_copy(i):
        return pltpu.make_async_remote_copy(
            src_ref=snd2.at[i],
            dst_ref=rcv2.at[e],
            send_sem=f_sem.at[0, i],
            recv_sem=f_sem.at[1, e],
            device_id=(dp_of(zl, jnp.int32(i // 2), c), 2 * x + i % 2),
            device_id_type=MESH,
        )

    for i in range(ne):
        mine = jnp.logical_and(x == i // 2, e == 2 * x + i % 2)

        @pl.when(mine)
        def _():
            rcv2[e] = snd2[i]

        @pl.when(jnp.logical_not(mine))
        def _():
            return_copy(i).start()

    for i in range(ne):

        @pl.when(jnp.logical_not(jnp.logical_and(to_self, e == i)))
        def _():
            arrived(rcv2.at[i], f_sem.at[1, i])

    home = rcv2[...].reshape(ne * 2 * CAP, feat).astype(BF16)
    mixed = gates_ref[:, 0:1] * dot(p0_out, home) + gates_ref[:, 1:2] * dot(p1_out, home)
    mixed_ref[...] = mixed.astype(BF16)
    gtok_ref[...] = dot(p0_grad + p1_grad, home).astype(BF16)

    for copy in sent:
        copy.wait_send()
    for i in range(ne):

        @pl.when(jnp.logical_not(jnp.logical_and(to_self, e == i)))
        def _():
            dispatch_copy(i).wait_send()

        @pl.when(jnp.logical_not(jnp.logical_and(x == i // 2, e == 2 * x + i % 2)))
        def _():
            return_copy(i).wait_send()

    for copy in loads:
        copy.wait()


def per_device(tokens, cotangent, route, gates, w_gate, w_up, w_down):
    nz = lax.axis_size("dp") // (NX * NC)
    ne = lax.axis_size("expert")
    feat = tokens.shape[1]
    chunk = 2 * feat
    hidden = w_gate.shape[1]
    rows = nz * NC * ROWS
    dma = pltpu.SemaphoreType.DMA
    vmem = pl.BlockSpec(memory_space=pltpu.VMEM)
    hbm = pl.BlockSpec(memory_space=pl.ANY)
    weight = jax.ShapeDtypeStruct(w_gate.shape, BF16)
    return pl.pallas_call(
        functools.partial(kernel, nz, ne),
        out_shape=(
            jax.ShapeDtypeStruct(tokens.shape, BF16),
            jax.ShapeDtypeStruct(tokens.shape, BF16),
            weight,
            weight,
            weight,
        ),
        in_specs=[vmem] * 4 + [hbm] * 3,
        out_specs=(vmem, vmem, hbm, hbm, hbm),
        scratch_shapes=[
            pltpu.VMEM((ne, 2 * CAP, feat), F32),
            pltpu.VMEM((ne, 2 * CAP, feat), F32),
            pltpu.VMEM((2, NX, NC, nz, ROWS, chunk), BF16),
            pltpu.VMEM((NX, hidden, chunk), BF16),
            pltpu.VMEM((NX, hidden, chunk), BF16),
            pltpu.VMEM((NX, hidden, chunk), BF16),
            pltpu.VMEM((3, rows, hidden), F32),
            pltpu.VMEM((3, rows, hidden), BF16),
            pltpu.VMEM((2, NX, NC, nz, ROWS, chunk), BF16),
            pltpu.VMEM((2, NX, nz, ROWS, chunk), BF16),
            pltpu.VMEM((2, nz, ROWS, chunk), BF16),
            pltpu.VMEM((2, 2, nz, ROWS, chunk), BF16),
            pltpu.VMEM((nz, 2, ROWS, chunk), BF16),
            pltpu.VMEM((nz, 2, ROWS, chunk), BF16),
            pltpu.VMEM((ne, 2 * CAP, feat), F32),
            pltpu.VMEM((ne, 2 * CAP, feat), F32),
            pltpu.VMEM((NX, hidden, chunk), BF16),
            pltpu.VMEM((NX, hidden, chunk), BF16),
            pltpu.VMEM((NX, hidden, chunk), BF16),
            dma((3 * NX,)),
            dma((3 * NX,)),
            dma((64,)),
            dma((2, ne)),
            dma((nz,)),
            dma((4, nz // 2)),
            dma((4, nz // 2)),
            dma((8,)),
            dma((nz,)),
            dma((2, ne)),
        ],
        compiler_params=pltpu.CompilerParams(
            collective_id=0, has_side_effects=True, vmem_limit_bytes=48 << 20
        ),
        name="expert_layer",
    )(tokens, cotangent, route, gates, w_gate, w_up, w_down)


def solution(mesh):
    return jax.shard_map(
        per_device,
        mesh=mesh,
        in_specs=(
            P("dp", "expert"),
            P("dp", "expert"),
            P("dp", None),
            P("dp", None),
            P("expert", "dp", None),
            P("expert", "dp", None),
            P("expert", "dp", None),
        ),
        out_specs=(
            P("dp", "expert"),
            P("dp", "expert"),
            P("expert", "dp", None),
            P("expert", "dp", None),
            P("expert", "dp", None),
        ),
        check_vma=False,
    )
```

time: 833 us -> 100 us (0.12)
  the two profiles are of different devices: /device:TPU:8 before, /device:TPU:62 now
where the time goes in v1:
time: 100 us; the launch traced here: 99.8 us
  Pallas kernels  91 us (91%)
  local copies, waits for them, and re-layouts  8.13 us (8%)
    pallas_call x1, Pallas kernels, per_device(): pl.pallas_call(functools.partial(kernel, nz, ne), out_shape=(jax.ShapeDty...  91 us
    unnamed x19, local copies, waits for them, and re-layouts  8.13 us

profile of v1, /device:TPU:62, one launch (start us, length us, event | category | flops | bytes accessed | tf_op | source)
XLA Modules:
  0.0 99.8 jit_solution(16628642481907301907)
XLA Ops:
  0.6 0.0 copy-start.5
  0.6 0.0 copy-start.4
  0.7 0.0 copy-start.3
  0.7 0.8 copy.12.route_ref
  1.4 0.0 copy-done.5
  1.4 0.1 copy.13.gates_ref
  1.5 0.0 copy-done.4
  1.5 0.0 copy-done.3
  1.5 0.0 copy-start
  1.6 1.1 %copy-done = bf16[1,192,2048]{2,1,0:T(8,128)(2,1)S(1)} copy-done((bf16[1,192,2048]{2,1,0:T(8,128)(2,1)S(1)}, bf16[1,192,2048]{2,1,0:T(8,128)(2,1)}, u32[]{:S(2)}) %copy-start) | copy-done | bytes 786456
  2.7 0.0 copy-start.1
  2.7 1.1 %copy-done.1 = bf16[1,192,2048]{2,1,0:T(8,128)(2,1)S(1)} copy-done((bf16[1,192,2048]{2,1,0:T(8,128)(2,1)S(1)}, bf16[1,192,2048]{2,1,0:T(8,128)(2,1)}, u32[]{:S(2)}) %copy-start.1) | copy-done | bytes 786456
  3.8 0.0 copy-start.2
  3.8 1.1 %copy-done.2 = bf16[1,192,2048]{2,1,0:T(8,128)(2,1)S(1)} copy-done((bf16[1,192,2048]{2,1,0:T(8,128)(2,1)S(1)}, bf16[1,192,2048]{2,1,0:T(8,128)(2,1)}, u32[]{:S(2)}) %copy-start.2) | copy-done | bytes 786456
  5.0 91.0 %expert_layer.1 = (bf16[12,256]{1,0:T(8,128)(2,1)S(1)}, bf16[12,256]{1,0:T(8,128)(2,1)S(1)}, bf16[1,192,2048]{2,1,0:T(8,128)(2,1)S(1)}, bf16[1,192,2048]{2,1,0:T(8,128)(2,1)S(1)}, bf16[1,192,2048]{2,1,0:T(8,128)(2,1)S(1)}) custom-call(bf16[12,256]{1,0:T(8,128)(2,1)S(1)} %copy-done.3, bf16[12,256]{1,0:T(8,128)(2,1)S(1)} %copy-done.4, ...), custom_call_target="tpu_custom_call" | custom-call | tf_op jit(solution)/shard_map/expert_layer/pallas_call | solution.py:408
  96.0 0.6 copy.19
  96.6 0.6 copy.20
  97.2 0.9 copy.21
  98.1 0.9 copy.22
  98.9 0.9 copy.23
Async XLA Ops:
  0.6 0.8 copy-start.5
  0.6 0.9 copy-start.4
  0.7 0.9 copy-start.3
  1.5 1.1 %copy-start = (bf16[1,192,2048]{2,1,0:T(8,128)(2,1)S(1)}, bf16[1,192,2048]{2,1,0:T(8,128)(2,1)}, u32[]{:S(2)}) copy-start(bf16[1,192,2048]{2,1,0:T(8,128)(2,1)} %wg_hbm.1) | copy-start | bytes 2359300
  2.7 1.1 %copy-start.1 = (bf16[1,192,2048]{2,1,0:T(8,128)(2,1)S(1)}, bf16[1,192,2048]{2,1,0:T(8,128)(2,1)}, u32[]{:S(2)}) copy-start(bf16[1,192,2048]{2,1,0:T(8,128)(2,1)} %wu_hbm.1) | copy-start | bytes 2359300
  3.8 1.1 %copy-start.2 = (bf16[1,192,2048]{2,1,0:T(8,128)(2,1)S(1)}, bf16[1,192,2048]{2,1,0:T(8,128)(2,1)}, u32[]{:S(2)}) copy-start(bf16[1,192,2048]{2,1,0:T(8,128)(2,1)} %wd_hbm.1) | copy-start | bytes 2359300

commit v2 on v1

v2 whole, which is shorter than its diff:
```python
import functools

import jax
import jax.numpy as jnp
from jax import lax
from jax.experimental import pallas as pl
from jax.experimental.pallas import tpu as pltpu
from jax.sharding import PartitionSpec as P

MESH = pl.DeviceIdType.MESH
BF16 = jnp.bfloat16
F32 = jnp.float32
NX = 4
NC = 2
NY = 4
NS = 2
NZ = 8
RING = NS * NZ
CAP = 4
ROWS = NX * CAP
QUAD = 4


def dot(left, right):
    return jnp.dot(left, right, preferred_element_type=F32)


def dot_cols(left, right):
    return lax.dot_general(left, right, (((1,), (1,)), ((), ())), preferred_element_type=F32)


def dot_rows(left, right):
    return lax.dot_general(left, right, (((0,), (0,)), ((), ())), preferred_element_type=F32)


def layer_kernel(
    tok_ref,
    cot_ref,
    route_ref,
    gates_ref,
    wg_hbm,
    wu_hbm,
    wd_hbm,
    mixed_ref,
    gtok_ref,
    gg_hbm,
    gu_hbm,
    gd_hbm,
    snd,
    rcv,
    uz,
    g,
    wg,
    wu,
    wd,
    hid,
    part,
    sib,
    xr,
    zbuf,
    rz,
    snd2,
    rcv2,
    gg,
    gu,
    gd,
    w_sem,
    o_sem,
    send_sem,
    d_sem,
    z_sem,
    x_sem,
    c_sem,
    s_sem,
    r_sem,
    q_sem,
    f_sem,
):
    p = lax.axis_index("dp")
    e = lax.axis_index("expert")
    zl = lax.div(p, NX * NC)
    x = lax.rem(lax.div(p, NC), NX)
    c = lax.rem(p, NC)
    zh = lax.div(e, NY)
    y = lax.rem(e, NY)
    ring = zh * NZ + zl
    other = 1 - c
    rows = NC * NZ * ROWS
    toks, feat = tok_ref.shape
    peers = [lax.rem(x + k, NX) for k in (1, 3, 2)]

    def device(xx, yy, cc):
        return (zl * (NX * NC) + xx * NC + cc, zh * NY + yy)

    def along_z(to):
        low = lax.rem(to, NZ)
        return (low * (NX * NC) + x * NC + c, lax.div(to, NZ) * NY + y)

    dev_peers = [device(xx, y, c) for xx in peers]
    dev_sib = device(x, y, other)
    sent = []

    def send(src, dst, rsem, to):
        copy = pltpu.make_async_remote_copy(
            src_ref=src,
            dst_ref=dst,
            send_sem=send_sem.at[len(sent)],
            recv_sem=rsem,
            device_id=to,
            device_id_type=MESH,
        )
        copy.start()
        sent.append(copy)

    def arrived(dst, rsem):
        pltpu.make_async_remote_copy(
            src_ref=dst,
            dst_ref=dst,
            send_sem=send_sem.at[0],
            recv_sem=rsem,
            device_id=dev_sib,
            device_id_type=MESH,
        ).wait_recv()

    barrier = pltpu.get_barrier_semaphore()

    def greet(to):
        pl.semaphore_signal(barrier, inc=1, device_id=to, device_id_type=MESH)

    around = []
    for d in range(1, RING // 2 + 1):
        around.append(lax.rem(ring + d, RING))
        if d < RING // 2:
            around.append(lax.rem(ring + RING - d, RING))
    for to in reversed(around):
        greet(along_z(to))
    diagonal = x == y
    for i in range(NY):

        @pl.when(jnp.logical_not(jnp.logical_and(diagonal, y == i)))
        def _():
            greet(device(y, jnp.int32(i), c))

        @pl.when(jnp.logical_not(jnp.logical_and(diagonal, x == i)))
        def _():
            greet(device(jnp.int32(i), x, c))

    for to in dev_peers:
        greet(to)
    greet(dev_sib)

    loads = []
    for n, (hbm, vmem) in enumerate(((wg_hbm, wg), (wu_hbm, wu), (wd_hbm, wd))):
        copy = pltpu.make_async_copy(hbm.at[0], vmem, w_sem.at[n])
        copy.start()
        loads.append(copy)

    lane = lax.broadcasted_iota(jnp.int32, (toks, NY * NS * 2 * CAP), 1)
    lane_e = ((lane >> 3) & 1) * NY + (lane >> 4)
    first = ((lane >> 2) & 1) == 0
    lane_c = (lane & 3).astype(F32)
    m0 = (route_ref[:, 0:1] == lane_e).astype(F32)
    m1 = (route_ref[:, 1:2] == lane_e).astype(F32)
    earlier = (
        lax.broadcasted_iota(jnp.int32, (toks, toks), 1)
        < lax.broadcasted_iota(jnp.int32, (toks, toks), 0)
    ).astype(F32)
    before = dot(earlier, m0 + m1)
    p0 = jnp.where(before == lane_c, m0, 0.0)
    p1 = jnp.where(before + m0 == lane_c, m1, 0.0)
    p0_out = jnp.where(first, p0, 0.0).astype(BF16)
    p1_out = jnp.where(first, p1, 0.0).astype(BF16)
    p0_grad = jnp.where(first, 0.0, p0).astype(BF16)
    p1_grad = jnp.where(first, 0.0, p1).astype(BF16)
    cot = cot_ref[...].astype(F32)
    weighted0 = (gates_ref[:, 0:1] * cot).astype(BF16)
    weighted1 = (gates_ref[:, 1:2] * cot).astype(BF16)
    placed = (
        dot_rows(p0_out + p1_out, tok_ref[...])
        + dot_rows(p0_grad, weighted0)
        + dot_rows(p1_grad, weighted1)
    )
    snd[...] = placed.reshape(NY, NS * 2 * CAP, feat)

    near = jnp.where(diagonal, 2 * NY - 2, 2 * NY)
    pl.semaphore_wait(barrier, near + (RING - 1) + (NX - 1) + 1)

    def dispatch_copy(i):
        return pltpu.make_async_remote_copy(
            src_ref=snd.at[i],
            dst_ref=rcv.at[x],
            send_sem=d_sem.at[0, i],
            recv_sem=d_sem.at[1, x],
            device_id=device(y, jnp.int32(i), c),
            device_id_type=MESH,
        )

    for i in range(NY):
        mine = jnp.logical_and(diagonal, y == i)

        @pl.when(mine)
        def _():
            rcv[x] = snd[i]

        @pl.when(jnp.logical_not(mine))
        def _():
            dispatch_copy(i).start()

    for i in range(NX):

        @pl.when(jnp.logical_not(jnp.logical_and(diagonal, x == i)))
        def _():
            arrived(rcv.at[i], d_sem.at[1, i])

    sub = lax.broadcasted_iota(jnp.int32, (2 * CAP, feat), 0) < CAP
    for s in range(NS):
        t = [rcv[i, 2 * CAP * s : 2 * CAP * (s + 1)] for i in range(NX)]
        r = [pltpu.roll(v, CAP, 0) for v in t]
        xs_rows = [jnp.where(sub, t[0], r[1]), jnp.where(sub, t[2], r[3])]
        dy_rows = [jnp.where(sub, r[0], t[1]), jnp.where(sub, r[2], t[3])]
        uz[s, 0] = jnp.concatenate(xs_rows, axis=0).astype(BF16)
        uz[s, 1] = jnp.concatenate(dy_rows, axis=0).astype(BF16)

    for to in around:
        send(uz.at[lax.div(to, NZ)], g.at[:, x, zh, c, zl], z_sem.at[ring], along_z(to))
    g[:, x, zh, c, zl] = uz[zh]

    q = lax.div(ring, QUAD)
    quads = [lax.rem(q + k, RING // QUAD) for k in (0, 1, 3, 2)]

    def span(n):
        return lax.div(quads[n], NS), pl.ds(QUAD * lax.rem(quads[n], NS), QUAD)

    def region(xi, cc, n):
        s, zs = span(n)
        return g.at[:, xi, s, cc, zs]

    def stage_a(n):
        for j in range(QUAD):
            if n == 0:
                if j == 0:
                    continue
                src = QUAD * q + lax.rem(ring + j, QUAD)
            else:
                src = QUAD * quads[n] + j
            arrived(g.at[:, x, lax.div(src, NZ), c, lax.rem(src, NZ)], z_sem.at[src])
        for i in range(NX - 1):
            send(region(x, c, n), region(x, c, n), x_sem.at[i, n], dev_peers[i])
        send(region(x, c, n), region(x, c, n), c_sem.at[NX - 1, n], dev_sib)

    sources = [peers[1], peers[0], peers[2]]

    def stage_b(n):
        for i in range(NX - 1):
            arrived(region(sources[i], c, n), x_sem.at[i, n])
            send(region(sources[i], c, n), region(sources[i], c, n), c_sem.at[i, n], dev_sib)

    nq = RING // QUAD
    for n in range(nq + 1):
        if n < nq:
            stage_a(n)
        if n >= 1:
            stage_b(n - 1)

    for copy in loads:
        copy.wait()
    for n in range(nq):
        for i in range(NX - 1):
            arrived(region(sources[i], other, n), c_sem.at[i, n])
        arrived(region(x, other, n), c_sem.at[NX - 1, n])

    def cols(xi, s):
        start = (s * NX + xi) * feat
        return slice(start, start + feat)

    def rows_of(a, xi, s):
        return g[a, xi, s].reshape(rows, feat)

    slices = [(xi, s) for xi in range(NX) for s in range(NS)]
    pre_gate = sum(dot_cols(rows_of(0, *i), wg[:, cols(*i)]) for i in slices)
    pre_up = sum(dot_cols(rows_of(0, *i), wu[:, cols(*i)]) for i in slices)
    grad_hidden = sum(dot_cols(rows_of(1, *i), wd[:, cols(*i)]) for i in slices)
    sig = jax.nn.sigmoid(pre_gate)
    silu = pre_gate * sig
    hid[0] = (silu * pre_up).astype(BF16)
    hid[1] = (grad_hidden * pre_up * sig * (1.0 + pre_gate * (1.0 - sig))).astype(BF16)
    hid[2] = (grad_hidden * silu).astype(BF16)

    for xi, s in slices:
        y0 = dot(hid[0], wd[:, cols(xi, s)])
        y1 = dot(hid[1], wg[:, cols(xi, s)]) + dot(hid[2], wu[:, cols(xi, s)])
        part[0, xi, s] = y0.astype(BF16).reshape(NC, NZ, ROWS, feat)
        part[1, xi, s] = y1.astype(BF16).reshape(NC, NZ, ROWS, feat)
    for n in reversed(range(nq)):
        s, zs = span(n)
        send(part.at[:, :, s, other, zs], sib.at[:, :, s, zs], s_sem.at[n], dev_sib)

    def chip_sum(xi, s, zs):
        return part[:, xi, s, c, zs].astype(F32) + sib[:, xi, s, zs].astype(F32)

    for n in reversed(range(nq)):
        s, zs = span(n)
        arrived(sib.at[:, :, s, zs], s_sem.at[n])
        for i in (2, 0, 1):
            xi = peers[i]
            part[:, xi, s, c, zs] = chip_sum(xi, s, zs).astype(BF16)
            send(part.at[:, xi, s, c, zs], xr.at[i, :, s, zs], r_sem.at[i, n], dev_peers[i])

    for xi, s in slices:
        gd[:, cols(xi, s)] = dot_rows(hid[0], rows_of(1, xi, s)).astype(BF16)
        gg[:, cols(xi, s)] = dot_rows(hid[1], rows_of(0, xi, s)).astype(BF16)
        gu[:, cols(xi, s)] = dot_rows(hid[2], rows_of(0, xi, s)).astype(BF16)
    stores = []
    for n, (vmem, hbm) in enumerate(((gd, gd_hbm), (gg, gg_hbm), (gu, gu_hbm))):
        copy = pltpu.make_async_copy(vmem, hbm.at[0], o_sem.at[n])
        copy.start()
        stores.append(copy)

    for n in reversed(range(nq)):
        s, zs = span(n)
        total = chip_sum(x, s, zs)
        for i in range(NX - 1):
            arrived(xr.at[i, :, s, zs], r_sem.at[i, n])
            total = total + xr[i, :, s, zs].astype(F32)
        for a in range(2):
            zbuf[pl.ds(QUAD * quads[n], QUAD), a] = total[a].astype(BF16)
        for j in range(QUAD):
            if n == 0:
                if j == 0:
                    continue
                to = QUAD * q + lax.rem(ring + j, QUAD)
            else:
                to = QUAD * quads[n] + j
            send(zbuf.at[to], rz.at[ring], q_sem.at[ring], along_z(to))
    rz[ring] = zbuf[ring]
    for src in around:
        arrived(rz.at[src], q_sem.at[src])

    for s in range(NS):
        total = rz[s * NZ].astype(F32)
        for z in range(1, NZ):
            total = total + rz[s * NZ + z].astype(F32)
        total = total.astype(BF16).astype(F32)
        block = slice(2 * CAP * s, 2 * CAP * (s + 1))
        for i in range(2):
            out_rows = total[0, 8 * i : 8 * i + 8]
            grad_rows = total[1, 8 * i : 8 * i + 8]
            snd2[2 * i, block] = jnp.where(sub, out_rows, pltpu.roll(grad_rows, CAP, 0))
            snd2[2 * i + 1, block] = jnp.where(sub, pltpu.roll(out_rows, CAP, 0), grad_rows)

    def return_copy(i):
        return pltpu.make_async_remote_copy(
            src_ref=snd2.at[i],
            dst_ref=rcv2.at[y],
            send_sem=f_sem.at[0, i],
            recv_sem=f_sem.at[1, y],
            device_id=device(jnp.int32(i), x, c),
            device_id_type=MESH,
        )

    for i in range(NX):
        mine = jnp.logical_and(diagonal, x == i)

        @pl.when(mine)
        def _():
            rcv2[y] = snd2[i]

        @pl.when(jnp.logical_not(mine))
        def _():
            return_copy(i).start()

    for i in range(NY):

        @pl.when(jnp.logical_not(jnp.logical_and(diagonal, y == i)))
        def _():
            arrived(rcv2.at[i], f_sem.at[1, i])

    home = rcv2[...].reshape(NY * NS * 2 * CAP, feat).astype(BF16)
    mixed = gates_ref[:, 0:1] * dot(p0_out, home) + gates_ref[:, 1:2] * dot(p1_out, home)
    mixed_ref[...] = mixed.astype(BF16)
    gtok_ref[...] = dot(p0_grad + p1_grad, home).astype(BF16)

    for copy in stores:
        copy.wait()
    for copy in sent:
        copy.wait_send()
    for i in range(NY):

        @pl.when(jnp.logical_not(jnp.logical_and(diagonal, y == i)))
        def _():
            dispatch_copy(i).wait_send()

        @pl.when(jnp.logical_not(jnp.logical_and(diagonal, x == i)))
        def _():
            return_copy(i).wait_send()


def store_kernel(n, *refs):
    copies = [
        pltpu.make_async_copy(refs[i], refs[n + i], refs[2 * n].at[i]) for i in range(n)
    ]
    for copy in copies:
        copy.start()
    for copy in copies:
        copy.wait()


def per_device(tokens, cotangent, route, gates, w_gate, w_up, w_down):
    assert lax.axis_size("dp") == NZ * NX * NC and lax.axis_size("expert") == NS * NY
    feat = tokens.shape[1]
    hidden = w_gate.shape[1]
    rows = NC * NZ * ROWS
    dma = pltpu.SemaphoreType.DMA
    vmem = pl.BlockSpec(memory_space=pltpu.VMEM)
    hbm = pl.BlockSpec(memory_space=pl.ANY)
    outs = (jax.ShapeDtypeStruct(tokens.shape, BF16),) * 2
    outs += (jax.ShapeDtypeStruct(w_gate.shape, BF16),) * 3
    nq = RING // QUAD
    results = pl.pallas_call(
        layer_kernel,
        out_shape=outs,
        in_specs=[vmem] * 4 + [hbm] * 3,
        out_specs=(vmem, vmem, hbm, hbm, hbm),
        scratch_shapes=[
            pltpu.VMEM((NY, NS * 2 * CAP, feat), F32),
            pltpu.VMEM((NX, NS * 2 * CAP, feat), F32),
            pltpu.VMEM((NS, 2, ROWS, feat), BF16),
            pltpu.VMEM((2, NX, NS, NC, NZ, ROWS, feat), BF16),
            pltpu.VMEM(w_gate.shape[1:], BF16),
            pltpu.VMEM(w_gate.shape[1:], BF16),
            pltpu.VMEM(w_gate.shape[1:], BF16),
            pltpu.VMEM((3, rows, hidden), BF16),
            pltpu.VMEM((2, NX, NS, NC, NZ, ROWS, feat), BF16),
            pltpu.VMEM((2, NX, NS, NZ, ROWS, feat), BF16),
            pltpu.VMEM((NX - 1, 2, NS, NZ, ROWS, feat), BF16),
            pltpu.VMEM((RING, 2, ROWS, feat), BF16),
            pltpu.VMEM((RING, 2, ROWS, feat), BF16),
            pltpu.VMEM((NX, NS * 2 * CAP, feat), F32),
            pltpu.VMEM((NY, NS * 2 * CAP, feat), F32),
            pltpu.VMEM(w_gate.shape[1:], BF16),
            pltpu.VMEM(w_gate.shape[1:], BF16),
            pltpu.VMEM(w_gate.shape[1:], BF16),
            dma((3,)),
            dma((3,)),
            dma((96,)),
            dma((2, NY)),
            dma((RING,)),
            dma((NX - 1, nq)),
            dma((NX, nq)),
            dma((nq,)),
            dma((NX - 1, nq)),
            dma((RING,)),
            dma((2, NY)),
        ],
        compiler_params=pltpu.CompilerParams(
            collective_id=0, has_side_effects=True, vmem_limit_bytes=62 << 20
        ),
        name="expert_layer",
    )(tokens, cotangent, route, gates, w_gate, w_up, w_down)
    return pl.pallas_call(
        functools.partial(store_kernel, len(outs)),
        out_shape=outs,
        in_specs=[hbm] * len(outs),
        out_specs=(hbm,) * len(outs),
        scratch_shapes=[dma((len(outs),))],
        compiler_params=pltpu.CompilerParams(vmem_limit_bytes=62 << 20),
        name="store_results",
    )(*results)


def solution(mesh):
    return jax.shard_map(
        per_device,
        mesh=mesh,
        in_specs=(
            P("dp", "expert"),
            P("dp", "expert"),
            P("dp", None),
            P("dp", None),
            P("expert", "dp", None),
            P("expert", "dp", None),
            P("expert", "dp", None),
        ),
        out_specs=(
            P("dp", "expert"),
            P("dp", "expert"),
            P("expert", "dp", None),
            P("expert", "dp", None),
            P("expert", "dp", None),
        ),
        check_vma=False,
    )
```

time: 100 us -> 150 us (1.50)
  the two profiles are of different devices: /device:TPU:62 before, /device:TPU:8 now
where the time goes in v2:
time: 150 us
  Pallas kernels  147 us (98%)
  local copies, waits for them, and re-layouts  2.05 us (1%)
    pallas_call x1, Pallas kernels, per_device(): pl.pallas_call(layer_kernel, out_shape=outs, in_specs=[vmem] * 4 + [hbm]...  73.9 us
    pallas_call x1, Pallas kernels, per_device(): pl.pallas_call(functools.partial(store_kernel, len(outs)), out_shape=outs...  73.1 us

profile of v2, /device:TPU:8, one launch (start us, length us, event | category | flops | bytes accessed | tf_op | source)
XLA Modules:
  0.0 149.7 jit_solution(5519151277324659762)
XLA Ops:
  0.6 0.0 copy-start
  0.6 1.4 copy.12.route_ref
  2.0 0.0 copy-done
  2.0 0.7 copy.13.gates_ref
  2.7 73.9 %expert_layer.1 = (bf16[12,256]{1,0:T(8,128)(2,1)}, bf16[12,256]{1,0:T(8,128)(2,1)}, bf16[1,192,2048]{2,1,0:T(8,128)(2,1)}, bf16[1,192,2048]{2,1,0:T(8,128)(2,1)}, bf16[1,192,2048]{2,1,0:T(8,128)(2,1)}) custom-call(bf16[12,256]{1,0:T(8,128)(2,1)} %tok_ref.1, bf16[12,256]{1,0:T(8,128)(2,1)} %cot_ref.1, s32[12,2]{1,0:T(8,128)} %copy.12.route_ref, ...), custom_call_target="tpu_custom_call" | custom-call | tf_op jit(solution)/shard_map/expert_layer/pallas_call | solution.py:419
  76.6 73.1 %store_results.1 = (bf16[12,256]{1,0:T(8,128)(2,1)}, bf16[12,256]{1,0:T(8,128)(2,1)}, bf16[1,192,2048]{2,1,0:T(8,128)(2,1)}, bf16[1,192,2048]{2,1,0:T(8,128)(2,1)}, bf16[1,192,2048]{2,1,0:T(8,128)(2,1)}) custom-call(bf16[12,256]{1,0:T(8,128)(2,1)} %get-tuple-element.10.refs_0_, bf16[12,256]{1,0:T(8,128)(2,1)} %get-tuple-element.11.refs_1_, ...), custom_call_target="tpu_custom_call" | custom-call | tf_op jit(solution)/shard_map/store_results/pallas_call | solution.py:460
Async XLA Ops:
  0.6 1.4 copy-start

commit v3 on v2

--- a/solution.py
+++ b/solution.py
@@ -155,31 +155,25 @@
         copy.start()
         loads.append(copy)
 
-    lane = lax.broadcasted_iota(jnp.int32, (toks, NY * NS * 2 * CAP), 1)
-    lane_e = ((lane >> 3) & 1) * NY + (lane >> 4)
-    first = ((lane >> 2) & 1) == 0
-    lane_c = (lane & 3).astype(F32)
-    m0 = (route_ref[:, 0:1] == lane_e).astype(F32)
-    m1 = (route_ref[:, 1:2] == lane_e).astype(F32)
+    picks = NY * NS * 2 * CAP
+    row = lax.broadcasted_iota(jnp.int32, (picks, toks), 0)
+    row_e = ((row >> 3) & 1) * NY + (row >> 4)
+    row_c = (row & 3).astype(F32)
+    m0 = (route_ref[0:1, :] == row_e).astype(F32)
+    m1 = (route_ref[1:2, :] == row_e).astype(F32)
     earlier = (
-        lax.broadcasted_iota(jnp.int32, (toks, toks), 1)
-        < lax.broadcasted_iota(jnp.int32, (toks, toks), 0)
+        lax.broadcasted_iota(jnp.int32, (toks, toks), 0)
+        < lax.broadcasted_iota(jnp.int32, (toks, toks), 1)
     ).astype(F32)
-    before = dot(earlier, m0 + m1)
-    p0 = jnp.where(before == lane_c, m0, 0.0)
-    p1 = jnp.where(before + m0 == lane_c, m1, 0.0)
-    p0_out = jnp.where(first, p0, 0.0).astype(BF16)
-    p1_out = jnp.where(first, p1, 0.0).astype(BF16)
-    p0_grad = jnp.where(first, 0.0, p0).astype(BF16)
-    p1_grad = jnp.where(first, 0.0, p1).astype(BF16)
-    cot = cot_ref[...].astype(F32)
-    weighted0 = (gates_ref[:, 0:1] * cot).astype(BF16)
-    weighted1 = (gates_ref[:, 1:2] * cot).astype(BF16)
-    placed = (
-        dot_rows(p0_out + p1_out, tok_ref[...])
-        + dot_rows(p0_grad, weighted0)
-        + dot_rows(p1_grad, weighted1)
-    )
+    before = dot(m0 + m1, earlier)
+    p0 = jnp.where(before == row_c, m0, 0.0)
+    p1 = jnp.where(before + m0 == row_c, m1, 0.0)
+    both = p0 + p1
+    gate = jnp.sum(p0 * gates_ref[0:1, :] + p1 * gates_ref[1:2, :], axis=1, keepdims=True)
+    first = ((lax.broadcasted_iota(jnp.int32, (picks, feat), 0) >> 2) & 1) == 0
+    pick = both.astype(BF16)
+    placed_grad = (gate * dot(pick, cot_ref[...])).astype(BF16).astype(F32)
+    placed = jnp.where(first, dot(pick, tok_ref[...]), placed_grad)
     snd[...] = placed.reshape(NY, NS * 2 * CAP, feat)
 
     near = jnp.where(diagonal, 2 * NY - 2, 2 * NY)
@@ -221,11 +215,23 @@
         uz[s, 0] = jnp.concatenate(xs_rows, axis=0).astype(BF16)
         uz[s, 1] = jnp.concatenate(dy_rows, axis=0).astype(BF16)
 
-    for to in around:
+    def send_unit(to):
         send(uz.at[lax.div(to, NZ)], g.at[:, x, zh, c, zl], z_sem.at[ring], along_z(to))
+
+    q = lax.div(ring, QUAD)
+    mates = [QUAD * q + lax.rem(ring + j, QUAD) for j in range(1, QUAD)]
+    across = lax.rem(ring + RING // 2, RING)
+    send_unit(across)
+    for to in mates:
+        send_unit(to)
+    for k in (1, 3):
+        for j in range(QUAD):
+            send_unit(QUAD * lax.rem(q + k, RING // QUAD) + lax.rem(ring + j, QUAD))
     g[:, x, zh, c, zl] = uz[zh]
 
-    q = lax.div(ring, QUAD)
+    def unit(src):
+        return g.at[:, x, lax.div(src, NZ), c, lax.rem(src, NZ)]
+
     quads = [lax.rem(q + k, RING // QUAD) for k in (0, 1, 3, 2)]
 
     def span(n):
@@ -235,15 +241,16 @@
         s, zs = span(n)
         return g.at[:, xi, s, cc, zs]
 
+    def pass_on():
+        arrived(unit(across), z_sem.at[across])
+        for to in mates:
+            send(unit(across), unit(across), z_sem.at[across], along_z(to))
+
     def stage_a(n):
         for j in range(QUAD):
-            if n == 0:
-                if j == 0:
-                    continue
-                src = QUAD * q + lax.rem(ring + j, QUAD)
-            else:
-                src = QUAD * quads[n] + j
-            arrived(g.at[:, x, lax.div(src, NZ), c, lax.rem(src, NZ)], z_sem.at[src])
+            src = QUAD * quads[n] + lax.rem(ring + j, QUAD)
+            if j > 0 or n in (1, 2):
+                arrived(unit(src), z_sem.at[src])
         for i in range(NX - 1):
             send(region(x, c, n), region(x, c, n), x_sem.at[i, n], dev_peers[i])
         send(region(x, c, n), region(x, c, n), c_sem.at[NX - 1, n], dev_sib)
@@ -256,11 +263,15 @@
             send(region(sources[i], c, n), region(sources[i], c, n), c_sem.at[i, n], dev_sib)
 
     nq = RING // QUAD
-    for n in range(nq + 1):
-        if n < nq:
-            stage_a(n)
-        if n >= 1:
-            stage_b(n - 1)
+    stage_a(0)
+    stage_a(1)
+    pass_on()
+    stage_b(0)
+    stage_a(2)
+    stage_b(1)
+    stage_a(3)
+    stage_b(2)
+    stage_b(3)
 
     for copy in loads:
         copy.wait()
@@ -375,10 +386,17 @@
         def _():
             arrived(rcv2.at[i], f_sem.at[1, i])
 
-    home = rcv2[...].reshape(NY * NS * 2 * CAP, feat).astype(BF16)
-    mixed = gates_ref[:, 0:1] * dot(p0_out, home) + gates_ref[:, 1:2] * dot(p1_out, home)
-    mixed_ref[...] = mixed.astype(BF16)
-    gtok_ref[...] = dot(p0_grad + p1_grad, home).astype(BF16)
+    home = rcv2[...].reshape(picks, feat)
+    out_pick = jnp.where(first[:, :toks], both, 0.0)
+    mixed_ref[...] = lax.dot_general(
+        out_pick,
+        gate * home,
+        (((0,), (0,)), ((), ())),
+        precision=lax.Precision.HIGHEST,
+        preferred_element_type=F32,
+    ).astype(BF16)
+    grad_pick = (both - out_pick).astype(BF16)
+    gtok_ref[...] = dot_rows(grad_pick, home.astype(BF16)).astype(BF16)
 
     for copy in stores:
         copy.wait()
@@ -396,12 +414,15 @@
 
 
 def store_kernel(n, *refs):
-    copies = [
-        pltpu.make_async_copy(refs[i], refs[n + i], refs[2 * n].at[i]) for i in range(n)
-    ]
-    for copy in copies:
+    ins, outs, bufs, (sems,) = refs[:n], refs[n : 2 * n], refs[2 * n : 3 * n], refs[3 * n :]
+    loads = [pltpu.make_async_copy(ins[i], bufs[i], sems.at[0, i]) for i in range(n)]
+    stores = [pltpu.make_async_copy(bufs[i], outs[i], sems.at[1, i]) for i in range(n)]
+    for copy in loads:
         copy.start()
-    for copy in copies:
+    for load, store in zip(loads, stores):
+        load.wait()
+        store.start()
+    for copy in stores:
         copy.wait()
 
 
@@ -456,13 +477,13 @@
             collective_id=0, has_side_effects=True, vmem_limit_bytes=62 << 20
         ),
         name="expert_layer",
-    )(tokens, cotangent, route, gates, w_gate, w_up, w_down)
+    )(tokens, cotangent, route.T, gates.T, w_gate, w_up, w_down)
     return pl.pallas_call(
         functools.partial(store_kernel, len(outs)),
         out_shape=outs,
         in_specs=[hbm] * len(outs),
         out_specs=(hbm,) * len(outs),
-        scratch_shapes=[dma((len(outs),))],
+        scratch_shapes=[pltpu.VMEM(out.shape, out.dtype) for out in outs] + [dma((2, len(outs)))],
         compiler_params=pltpu.CompilerParams(vmem_limit_bytes=62 << 20),
         name="store_results",
     )(*results)

time: 150 us -> 76.1 us (0.51)
  the two profiles are of different devices: /device:TPU:8 before, /device:TPU:4 now
where the time goes in v3:
time: 76.1 us; the launch traced here: 75.8 us
  Pallas kernels  75.2 us (99%)
    pallas_call x1, Pallas kernels, per_device(): pl.pallas_call(layer_kernel, out_shape=outs, in_specs=[vmem] * 4 + [hbm]...  72.5 us
    pallas_call x1, Pallas kernels, per_device(): pl.pallas_call(functools.partial(store_kernel, len(outs)), out_shape=outs...  2.65 us

profile of v3, /device:TPU:4, one launch (start us, length us, event | category | flops | bytes accessed | tf_op | source)
XLA Modules:
  0.0 75.8 jit_solution(14056205733979773943)
XLA Ops:
  0.6 72.5 %expert_layer.1 = (bf16[12,256]{1,0:T(8,128)(2,1)}, bf16[12,256]{1,0:T(8,128)(2,1)}, bf16[1,192,2048]{2,1,0:T(8,128)(2,1)}, bf16[1,192,2048]{2,1,0:T(8,128)(2,1)}, bf16[1,192,2048]{2,1,0:T(8,128)(2,1)}) custom-call(bf16[12,256]{1,0:T(8,128)(2,1)} %tok_ref.1, bf16[12,256]{1,0:T(8,128)(2,1)} %cot_ref.1, s32[2,12]{1,0:T(2,128)} %bitcast.2, f32[2,12]{1,0:T(2,128)} %bitcast.3, ...), custom_call_target="tpu_custom_call" | custom-call | tf_op jit(solution)/shard_map/expert_layer/pallas_call | solution.py:440
  73.1 2.7 %store_results.1 = (bf16[12,256]{1,0:T(8,128)(2,1)}, bf16[12,256]{1,0:T(8,128)(2,1)}, bf16[1,192,2048]{2,1,0:T(8,128)(2,1)}, bf16[1,192,2048]{2,1,0:T(8,128)(2,1)}, bf16[1,192,2048]{2,1,0:T(8,128)(2,1)}) custom-call(bf16[12,256]{1,0:T(8,128)(2,1)} %get-tuple-element.10.refs_0_, bf16[12,256]{1,0:T(8,128)(2,1)} %get-tuple-element.11.refs_1_, ...), custom_call_target="tpu_custom_call" | custom-call | tf_op jit(solution)/shard_map/store_results/pallas_call | solution.py:481

commit v4 on v3

--- a/solution.py
+++ b/solution.py
@@ -75,6 +75,7 @@
     r_sem,
     q_sem,
     f_sem,
+    vouch,
 ):
     p = lax.axis_index("dp")
     e = lax.axis_index("expert")
@@ -127,12 +128,11 @@
     def greet(to):
         pl.semaphore_signal(barrier, inc=1, device_id=to, device_id_type=MESH)
 
-    around = []
-    for d in range(1, RING // 2 + 1):
-        around.append(lax.rem(ring + d, RING))
-        if d < RING // 2:
-            around.append(lax.rem(ring + RING - d, RING))
-    for to in reversed(around):
+    around = [lax.rem(ring + k, RING) for k in range(1, RING)]
+    q = lax.div(ring, QUAD)
+    mates = [QUAD * q + lax.rem(ring + j, QUAD) for j in range(1, QUAD)]
+    across = [lax.rem(ring + k * QUAD, RING) for k in (2, 1, 3)]
+    for to in across[1:] + mates:
         greet(along_z(to))
     diagonal = x == y
     for i in range(NY):
@@ -177,7 +177,9 @@
     snd[...] = placed.reshape(NY, NS * 2 * CAP, feat)
 
     near = jnp.where(diagonal, 2 * NY - 2, 2 * NY)
-    pl.semaphore_wait(barrier, near + (RING - 1) + (NX - 1) + 1)
+    pl.semaphore_wait(barrier, near + 2 + (QUAD - 1) + (NX - 1) + 1)
+
+    pl.semaphore_signal(vouch, inc=1, device_id=along_z(across[2]), device_id_type=MESH)
 
     def dispatch_copy(i):
         return pltpu.make_async_remote_copy(
@@ -218,15 +220,10 @@
     def send_unit(to):
         send(uz.at[lax.div(to, NZ)], g.at[:, x, zh, c, zl], z_sem.at[ring], along_z(to))
 
-    q = lax.div(ring, QUAD)
-    mates = [QUAD * q + lax.rem(ring + j, QUAD) for j in range(1, QUAD)]
-    across = lax.rem(ring + RING // 2, RING)
-    send_unit(across)
-    for to in mates:
+    for to in across[1:] + mates:
         send_unit(to)
-    for k in (1, 3):
-        for j in range(QUAD):
-            send_unit(QUAD * lax.rem(q + k, RING // QUAD) + lax.rem(ring + j, QUAD))
+    pl.semaphore_wait(vouch, 1)
+    send_unit(across[0])
     g[:, x, zh, c, zl] = uz[zh]
 
     def unit(src):
@@ -237,48 +234,57 @@
     def span(n):
         return lax.div(quads[n], NS), pl.ds(QUAD * lax.rem(quads[n], NS), QUAD)
 
-    def region(xi, cc, n):
+    def pass_on(src):
+        arrived(unit(src), z_sem.at[src])
+        for to in mates:
+            send(unit(src), unit(src), z_sem.at[src], along_z(to))
+
+    def fan(ref, n):
+        for i in range(NX - 1):
+            send(ref(x), ref(x), x_sem.at[i, n], dev_peers[i])
+
+    def unit_of(src):
+        s, z = lax.div(src, NZ), lax.rem(src, NZ)
+        return lambda xi: g.at[:, xi, s, c, z]
+
+    def quad_of(n, cc):
         s, zs = span(n)
-        return g.at[:, xi, s, cc, zs]
-
-    def pass_on():
-        arrived(unit(across), z_sem.at[across])
-        for to in mates:
-            send(unit(across), unit(across), z_sem.at[across], along_z(to))
-
-    def stage_a(n):
-        for j in range(QUAD):
+        return lambda xi: g.at[:, xi, s, cc, zs]
+
+    nq = RING // QUAD
+    groups = [quad_of(0, c)]
+    for src in mates:
+        arrived(unit(src), z_sem.at[src])
+    fan(groups[0], 0)
+
+    def forward(src):
+        fan(unit_of(src), len(groups))
+        groups.append(unit_of(src))
+
+    for src in (across[1], across[2], across[0]):
+        pass_on(src)
+        forward(src)
+    for n in (1, 2, 3):
+        for j in range(1, QUAD):
             src = QUAD * quads[n] + lax.rem(ring + j, QUAD)
-            if j > 0 or n in (1, 2):
-                arrived(unit(src), z_sem.at[src])
-        for i in range(NX - 1):
-            send(region(x, c, n), region(x, c, n), x_sem.at[i, n], dev_peers[i])
-        send(region(x, c, n), region(x, c, n), c_sem.at[NX - 1, n], dev_sib)
+            arrived(unit(src), z_sem.at[src])
+            forward(src)
 
     sources = [peers[1], peers[0], peers[2]]
-
-    def stage_b(n):
-        for i in range(NX - 1):
-            arrived(region(sources[i], c, n), x_sem.at[i, n])
-            send(region(sources[i], c, n), region(sources[i], c, n), c_sem.at[i, n], dev_sib)
-
-    nq = RING // QUAD
-    stage_a(0)
-    stage_a(1)
-    pass_on()
-    stage_b(0)
-    stage_a(2)
-    stage_b(1)
-    stage_a(3)
-    stage_b(2)
-    stage_b(3)
+    for n in range(nq):
+        s, zs = span(n)
+        members = {0: [0], 1: [1, 4, 5, 6], 2: [2, 7, 8, 9], 3: [3, 10, 11, 12]}[n]
+        for m in members:
+            for i in range(NX - 1):
+                arrived(groups[m](sources[i]), x_sem.at[i, m])
+        whole = g.at[:, :, s, c, zs]
+        send(whole, whole, c_sem.at[n], dev_sib)
 
     for copy in loads:
         copy.wait()
     for n in range(nq):
-        for i in range(NX - 1):
-            arrived(region(sources[i], other, n), c_sem.at[i, n])
-        arrived(region(x, other, n), c_sem.at[NX - 1, n])
+        s, zs = span(n)
+        arrived(g.at[:, :, s, other, zs], c_sem.at[n])
 
     def cols(xi, s):
         start = (s * NX + xi) * feat
@@ -466,12 +472,13 @@
             dma((96,)),
             dma((2, NY)),
             dma((RING,)),
-            dma((NX - 1, nq)),
-            dma((NX, nq)),
+            dma((NX - 1, 13)),
+            dma((nq,)),
             dma((nq,)),
             dma((NX - 1, nq)),
             dma((RING,)),
             dma((2, NY)),
+            pltpu.SemaphoreType.REGULAR,
         ],
         compiler_params=pltpu.CompilerParams(
             collective_id=0, has_side_effects=True, vmem_limit_bytes=62 << 20

time: 76.1 us -> 70.1 us (0.921)
  Pallas kernels: 75.2 us -> 69.2 us
    pallas_call x1, Pallas kernels: 72.5 us -> 66.5 us  [per_device(): pl.pallas_call(layer_kernel, out_shape=outs, in_specs=[vmem] * 4 + [hbm]...]
where the time goes in v4:
time: 70.1 us; the launch traced here: 69.8 us
  Pallas kernels  69.2 us (99%)
    pallas_call x1, Pallas kernels, per_device(): pl.pallas_call(layer_kernel, out_shape=outs, in_specs=[vmem] * 4 + [hbm]...  66.5 us
    pallas_call x1, Pallas kernels, per_device(): pl.pallas_call(functools.partial(store_kernel, len(outs)), out_shape=outs...  2.65 us

profile of v4, /device:TPU:4, one launch (start us, length us, event | category | flops | bytes accessed | tf_op | source)
XLA Modules:
  0.0 69.8 jit_solution(2759406406053514288)
XLA Ops:
  0.6 66.5 %expert_layer.1 = (bf16[12,256]{1,0:T(8,128)(2,1)}, bf16[12,256]{1,0:T(8,128)(2,1)}, bf16[1,192,2048]{2,1,0:T(8,128)(2,1)}, bf16[1,192,2048]{2,1,0:T(8,128)(2,1)}, bf16[1,192,2048]{2,1,0:T(8,128)(2,1)}) custom-call(bf16[12,256]{1,0:T(8,128)(2,1)} %tok_ref.1, bf16[12,256]{1,0:T(8,128)(2,1)} %cot_ref.1, s32[2,12]{1,0:T(2,128)} %bitcast.2, f32[2,12]{1,0:T(2,128)} %bitcast.3, ...), custom_call_target="tpu_custom_call" | custom-call | tf_op jit(solution)/shard_map/expert_layer/pallas_call | solution.py:446
  67.2 2.7 %store_results.1 = (bf16[12,256]{1,0:T(8,128)(2,1)}, bf16[12,256]{1,0:T(8,128)(2,1)}, bf16[1,192,2048]{2,1,0:T(8,128)(2,1)}, bf16[1,192,2048]{2,1,0:T(8,128)(2,1)}, bf16[1,192,2048]{2,1,0:T(8,128)(2,1)}) custom-call(bf16[12,256]{1,0:T(8,128)(2,1)} %get-tuple-element.10.refs_0_, bf16[12,256]{1,0:T(8,128)(2,1)} %get-tuple-element.11.refs_1_, ...), custom_call_target="tpu_custom_call" | custom-call | tf_op jit(solution)/shard_map/store_results/pallas_call | solution.py:488

commit v5 on v4

--- a/solution.py
+++ b/solution.py
@@ -19,6 +19,7 @@
 CAP = 4
 ROWS = NX * CAP
 QUAD = 4
+PIECES = 4
 
 
 def dot(left, right):
@@ -34,10 +35,10 @@
 
 
 def layer_kernel(
-    tok_ref,
-    cot_ref,
-    route_ref,
-    gates_ref,
+    tok_hbm,
+    cot_hbm,
+    route_hbm,
+    gates_hbm,
     wg_hbm,
     wu_hbm,
     wd_hbm,
@@ -46,6 +47,10 @@
     gg_hbm,
     gu_hbm,
     gd_hbm,
+    tok_ref,
+    cot_ref,
+    route_ref,
+    gates_ref,
     snd,
     rcv,
     uz,
@@ -64,6 +69,7 @@
     gg,
     gu,
     gd,
+    i_sem,
     w_sem,
     o_sem,
     send_sem,
@@ -149,11 +155,27 @@
         greet(to)
     greet(dev_sib)
 
+    tables = [
+        pltpu.make_async_copy(hbm, vmem, i_sem.at[n])
+        for n, (hbm, vmem) in enumerate(
+            (
+                (route_hbm, route_ref),
+                (gates_hbm, gates_ref),
+                (tok_hbm, tok_ref),
+                (cot_hbm, cot_ref),
+            )
+        )
+    ]
+    for copy in tables:
+        copy.start()
     loads = []
     for n, (hbm, vmem) in enumerate(((wg_hbm, wg), (wu_hbm, wu), (wd_hbm, wd))):
         copy = pltpu.make_async_copy(hbm.at[0], vmem, w_sem.at[n])
         copy.start()
         loads.append(copy)
+
+    for copy in tables:
+        copy.wait()
 
     picks = NY * NS * 2 * CAP
     row = lax.broadcasted_iota(jnp.int32, (picks, toks), 0)
@@ -323,15 +345,17 @@
             part[:, xi, s, c, zs] = chip_sum(xi, s, zs).astype(BF16)
             send(part.at[:, xi, s, c, zs], xr.at[i, :, s, zs], r_sem.at[i, n], dev_peers[i])
 
-    for xi, s in slices:
-        gd[:, cols(xi, s)] = dot_rows(hid[0], rows_of(1, xi, s)).astype(BF16)
-        gg[:, cols(xi, s)] = dot_rows(hid[1], rows_of(0, xi, s)).astype(BF16)
-        gu[:, cols(xi, s)] = dot_rows(hid[2], rows_of(0, xi, s)).astype(BF16)
     stores = []
-    for n, (vmem, hbm) in enumerate(((gd, gd_hbm), (gg, gg_hbm), (gu, gu_hbm))):
-        copy = pltpu.make_async_copy(vmem, hbm.at[0], o_sem.at[n])
+
+    def weight_grad(k, a, out, hbm):
+        across_rows = hid[k].astype(F32).T.astype(BF16)
+        for xi, s in slices:
+            out[:, cols(xi, s)] = dot(across_rows, rows_of(a, xi, s)).astype(BF16)
+        copy = pltpu.make_async_copy(out, hbm.at[0], o_sem.at[k])
         copy.start()
         stores.append(copy)
+
+    weight_grad(0, 1, gd, gd_hbm)
 
     for n in reversed(range(nq)):
         s, zs = span(n)
@@ -350,6 +374,8 @@
                 to = QUAD * quads[n] + j
             send(zbuf.at[to], rz.at[ring], q_sem.at[ring], along_z(to))
     rz[ring] = zbuf[ring]
+    weight_grad(1, 0, gg, gg_hbm)
+    weight_grad(2, 0, gu, gu_hbm)
     for src in around:
         arrived(rz.at[src], q_sem.at[src])
 
@@ -421,8 +447,18 @@
 
 def store_kernel(n, *refs):
     ins, outs, bufs, (sems,) = refs[:n], refs[n : 2 * n], refs[2 * n : 3 * n], refs[3 * n :]
-    loads = [pltpu.make_async_copy(ins[i], bufs[i], sems.at[0, i]) for i in range(n)]
-    stores = [pltpu.make_async_copy(bufs[i], outs[i], sems.at[1, i]) for i in range(n)]
+    loads, stores = [], []
+    for i in range(n):
+        shape = ins[i].shape
+        for j in range(PIECES if len(shape) == 3 else 1):
+            k = len(loads)
+            if len(shape) == 3:
+                rows = shape[1] // PIECES
+                at = (0, pl.ds(j * rows, rows))
+            else:
+                at = (slice(None),)
+            loads.append(pltpu.make_async_copy(ins[i].at[at], bufs[i].at[at], sems.at[0, k]))
+            stores.append(pltpu.make_async_copy(bufs[i].at[at], outs[i].at[at], sems.at[1, k]))
     for copy in loads:
         copy.start()
     for load, store in zip(loads, stores):
@@ -446,9 +482,13 @@
     results = pl.pallas_call(
         layer_kernel,
         out_shape=outs,
-        in_specs=[vmem] * 4 + [hbm] * 3,
+        in_specs=[hbm] * 7,
         out_specs=(vmem, vmem, hbm, hbm, hbm),
         scratch_shapes=[
+            pltpu.VMEM(tokens.shape, BF16),
+            pltpu.VMEM(tokens.shape, BF16),
+            pltpu.VMEM(route.shape[::-1], route.dtype),
+            pltpu.VMEM(route.shape[::-1], gates.dtype),
             pltpu.VMEM((NY, NS * 2 * CAP, feat), F32),
             pltpu.VMEM((NX, NS * 2 * CAP, feat), F32),
             pltpu.VMEM((NS, 2, ROWS, feat), BF16),
@@ -467,6 +507,7 @@
             pltpu.VMEM(w_gate.shape[1:], BF16),
             pltpu.VMEM(w_gate.shape[1:], BF16),
             pltpu.VMEM(w_gate.shape[1:], BF16),
+            dma((4,)),
             dma((3,)),
             dma((3,)),
             dma((96,)),
@@ -490,7 +531,7 @@
         out_shape=outs,
         in_specs=[hbm] * len(outs),
         out_specs=(hbm,) * len(outs),
-        scratch_shapes=[pltpu.VMEM(out.shape, out.dtype) for out in outs] + [dma((2, len(outs)))],
+        scratch_shapes=[pltpu.VMEM(out.shape, out.dtype) for out in outs] + [dma((2, 3 * PIECES + 2))],
         compiler_params=pltpu.CompilerParams(vmem_limit_bytes=62 << 20),
         name="store_results",
     )(*results)

time: 70.1 us -> 69.6 us (level)
  no operation moved by 1% of the time
where the time goes in v5:
time: 69.6 us; the launch traced here: 69.4 us
  Pallas kernels  68.8 us (99%)
    pallas_call x1, Pallas kernels, per_device(): pl.pallas_call(layer_kernel, out_shape=outs, in_specs=[hbm] * 7, out_spec...  66.1 us
    pallas_call x1, Pallas kernels, per_device(): pl.pallas_call(functools.partial(store_kernel, len(outs)), out_shape=outs...  2.68 us

profile of v5, /device:TPU:4, one launch (start us, length us, event | category | flops | bytes accessed | tf_op | source)
XLA Modules:
  0.0 69.4 jit_solution(12253277982708268250)
XLA Ops:
  0.6 66.1 %expert_layer.1 = (bf16[12,256]{1,0:T(8,128)(2,1)}, bf16[12,256]{1,0:T(8,128)(2,1)}, bf16[1,192,2048]{2,1,0:T(8,128)(2,1)}, bf16[1,192,2048]{2,1,0:T(8,128)(2,1)}, bf16[1,192,2048]{2,1,0:T(8,128)(2,1)}) custom-call(bf16[12,256]{1,0:T(8,128)(2,1)} %tok_hbm.1, bf16[12,256]{1,0:T(8,128)(2,1)} %cot_hbm.1, s32[2,12]{1,0:T(2,128)} %bitcast.2, f32[2,12]{1,0:T(2,128)} %bitcast.3, ...), custom_call_target="tpu_custom_call" | custom-call | tf_op jit(solution)/shard_map/expert_layer/pallas_call | solution.py:482
  66.7 2.7 %store_results.1 = (bf16[12,256]{1,0:T(8,128)(2,1)}, bf16[12,256]{1,0:T(8,128)(2,1)}, bf16[1,192,2048]{2,1,0:T(8,128)(2,1)}, bf16[1,192,2048]{2,1,0:T(8,128)(2,1)}, bf16[1,192,2048]{2,1,0:T(8,128)(2,1)}) custom-call(bf16[12,256]{1,0:T(8,128)(2,1)} %get-tuple-element.10.refs_0_, bf16[12,256]{1,0:T(8,128)(2,1)} %get-tuple-element.11.refs_1_, ...), custom_call_target="tpu_custom_call" | custom-call | tf_op jit(solution)/shard_map/store_results/pallas_call | solution.py:529

commit v6 on v5

--- a/solution.py
+++ b/solution.py
@@ -42,8 +42,8 @@
     wg_hbm,
     wu_hbm,
     wd_hbm,
-    mixed_ref,
-    gtok_ref,
+    mixed_hbm,
+    gtok_hbm,
     gg_hbm,
     gu_hbm,
     gd_hbm,
@@ -51,6 +51,8 @@
     cot_ref,
     route_ref,
     gates_ref,
+    mixed_ref,
+    gtok_ref,
     snd,
     rcv,
     uz,
@@ -412,6 +414,8 @@
         def _():
             return_copy(i).start()
 
+    for copy in sent:
+        copy.wait_send()
     for i in range(NY):
 
         @pl.when(jnp.logical_not(jnp.logical_and(diagonal, y == i)))
@@ -429,11 +433,13 @@
     ).astype(BF16)
     grad_pick = (both - out_pick).astype(BF16)
     gtok_ref[...] = dot_rows(grad_pick, home.astype(BF16)).astype(BF16)
+    for n, (vmem, hbm) in enumerate(((mixed_ref, mixed_hbm), (gtok_ref, gtok_hbm))):
+        copy = pltpu.make_async_copy(vmem, hbm, o_sem.at[3 + n])
+        copy.start()
+        stores.append(copy)
 
     for copy in stores:
         copy.wait()
-    for copy in sent:
-        copy.wait_send()
     for i in range(NY):
 
         @pl.when(jnp.logical_not(jnp.logical_and(diagonal, y == i)))
@@ -474,7 +480,6 @@
     hidden = w_gate.shape[1]
     rows = NC * NZ * ROWS
     dma = pltpu.SemaphoreType.DMA
-    vmem = pl.BlockSpec(memory_space=pltpu.VMEM)
     hbm = pl.BlockSpec(memory_space=pl.ANY)
     outs = (jax.ShapeDtypeStruct(tokens.shape, BF16),) * 2
     outs += (jax.ShapeDtypeStruct(w_gate.shape, BF16),) * 3
@@ -483,12 +488,14 @@
         layer_kernel,
         out_shape=outs,
         in_specs=[hbm] * 7,
-        out_specs=(vmem, vmem, hbm, hbm, hbm),
+        out_specs=(hbm,) * 5,
         scratch_shapes=[
             pltpu.VMEM(tokens.shape, BF16),
             pltpu.VMEM(tokens.shape, BF16),
             pltpu.VMEM(route.shape[::-1], route.dtype),
             pltpu.VMEM(route.shape[::-1], gates.dtype),
+            pltpu.VMEM(tokens.shape, BF16),
+            pltpu.VMEM(tokens.shape, BF16),
             pltpu.VMEM((NY, NS * 2 * CAP, feat), F32),
             pltpu.VMEM((NX, NS * 2 * CAP, feat), F32),
             pltpu.VMEM((NS, 2, ROWS, feat), BF16),
@@ -509,7 +516,7 @@
             pltpu.VMEM(w_gate.shape[1:], BF16),
             dma((4,)),
             dma((3,)),
-            dma((3,)),
+            dma((5,)),
             dma((96,)),
             dma((2, NY)),
             dma((RING,)),

time: 69.6 us -> 69.5 us (level)
  no operation moved by 1% of the time
where the time goes in v6:
time: 69.5 us; the launch traced here: 69.3 us
  Pallas kernels  68.6 us (99%)
    pallas_call x1, Pallas kernels, per_device(): pl.pallas_call(layer_kernel, out_shape=outs, in_specs=[hbm] * 7, out_spec...  66 us
    pallas_call x1, Pallas kernels, per_device(): pl.pallas_call(functools.partial(store_kernel, len(outs)), out_shape=outs...  2.68 us

profile of v6, /device:TPU:4, one launch (start us, length us, event | category | flops | bytes accessed | tf_op | source)
XLA Modules:
  0.0 69.3 jit_solution(15902331913656310766)
XLA Ops:
  0.6 66.0 %expert_layer.1 = (bf16[12,256]{1,0:T(8,128)(2,1)}, bf16[12,256]{1,0:T(8,128)(2,1)}, bf16[1,192,2048]{2,1,0:T(8,128)(2,1)}, bf16[1,192,2048]{2,1,0:T(8,128)(2,1)}, bf16[1,192,2048]{2,1,0:T(8,128)(2,1)}) custom-call(bf16[12,256]{1,0:T(8,128)(2,1)} %tok_hbm.1, bf16[12,256]{1,0:T(8,128)(2,1)} %cot_hbm.1, s32[2,12]{1,0:T(2,128)} %bitcast.2, f32[2,12]{1,0:T(2,128)} %bitcast.3, ...), custom_call_target="tpu_custom_call" | custom-call | tf_op jit(solution)/shard_map/expert_layer/pallas_call | solution.py:487
  66.6 2.7 %store_results.1 = (bf16[12,256]{1,0:T(8,128)(2,1)}, bf16[12,256]{1,0:T(8,128)(2,1)}, bf16[1,192,2048]{2,1,0:T(8,128)(2,1)}, bf16[1,192,2048]{2,1,0:T(8,128)(2,1)}, bf16[1,192,2048]{2,1,0:T(8,128)(2,1)}) custom-call(bf16[12,256]{1,0:T(8,128)(2,1)} %get-tuple-element.10.refs_0_, bf16[12,256]{1,0:T(8,128)(2,1)} %get-tuple-element.11.refs_1_, ...), custom_call_target="tpu_custom_call" | custom-call | tf_op jit(solution)/shard_map/store_results/pallas_call | solution.py:536
